TPU v7x, 32 devices: a whole 2x2x4 slice. The times are simulated.
32 devices in a mesh: dir: 8 (over y, x, core), freq: 4 (over z).
Axes of the slice: x: 2, y: 2, z: 4, core: 2. Of those that a mesh axis runs over, the one named last changes fastest.
Arguments:
- observed: float32 [512, 8, 2, 2, 512], P('dir', 'freq'), as said below
- flags: int32 [512, 2, 512], P('dir'), may hold values from 0 to 1, as said below
- screen: float32 [16, 512], P('dir'), may hold values from -6 to 6
- screen_kernel: float32 [512, 512], replicated
- station_uv: float32 [2, 2, 512], replicated, may hold values from -360 to 360
- source_lm: float32 [2, 3072], P(None, 'dir'), may hold values from -0.05 to 0.05
- source_flux: float32 [3072], P('dir')
- station_gain: bfloat16 [8, 2, 2, 512, 3072], P('freq', None, None, None, 'dir'), may hold values from -4.1875 to 4.1875
- source_direction: int32 [3072], P('dir'), may hold values from 0 to 1
- freq_ratio: float32 [8], P('freq')
Outputs:
- residual: float32 [512, 8, 2, 2, 512], P('dir', 'freq')
- updated_screen: float32 [16, 512], P('dir')
Inputs may be any that keep to these rules, and one draw needn't show every extreme that they name: observed is Hermitian in its stations: observed[p, f, t, 0, q] equals observed[q, f, t, 0, p] and observed[p, f, t, 1, q] equals minus observed[q, f, t, 1, p]. flags[p, t, q] equals flags[q, t, p].
All inputs are finite; a program needn't handle non-finite values.
Results may differ from a plain program's by a relative error of at most 0.0037.
Values may be sent and summed in bfloat16 or wider, within the bound.
A program may use at most 128 MiB of HBM per device.

v0:
```python
import math

import jax
import jax.numpy as jnp
from jax import lax
from jax.sharding import PartitionSpec as P

step_size = 0.3
epsilon = 1e-06
highest = lax.Precision.HIGHEST


def body(
    observed,
    flags,
    screen,
    screen_kernel,
    station_uv,
    source_lm,
    source_flux,
    station_gain,
    source_direction,
    freq_ratio,
):
    dir_count = lax.axis_size("dir")
    stations = screen.shape[1]
    local_dirs = screen.shape[0]
    local_sources = source_flux.shape[0]
    local_rows = observed.shape[0]
    channels = freq_ratio.shape[0]
    times_count = station_uv.shape[0]
    matrices = channels * times_count
    scaling = 1.0 / math.sqrt(local_sources * dir_count)
    onehot_dirs = (
        source_direction[:, None] == jnp.arange(local_dirs, dtype=jnp.int32)[None, :]
    ).astype(jnp.float32)
    screen_src = jnp.einsum("dp,kd->pk", screen, onehot_dirs, precision=highest)
    freq_each = jnp.repeat(freq_ratio, times_count)
    uv_each = jnp.tile(station_uv, (channels, 1, 1))
    geometry = jnp.einsum("mcp,ck->pmk", uv_each, source_lm, precision=highest)
    phase_angle = (
        screen_src[:, None, :] / freq_each[None, :, None]
        + (2.0 * math.pi * freq_each)[None, :, None] * geometry
    )
    gain_all = station_gain.reshape(matrices, 2, stations, local_sources).astype(jnp.float32)
    gain_re = jnp.transpose(gain_all[:, 0], (1, 0, 2))
    gain_im = jnp.transpose(gain_all[:, 1], (1, 0, 2))
    cosine = jnp.cos(phase_angle)
    sine = jnp.sin(phase_angle)
    amplitude = jnp.sqrt(source_flux)[None, None, :]
    phasor_re = (amplitude * (gain_re * cosine - gain_im * sine)).astype(jnp.bfloat16)
    phasor_im = (amplitude * (gain_re * sine + gain_im * cosine)).astype(jnp.bfloat16)
    left_mat = jnp.concatenate([phasor_re, phasor_im], axis=2)
    skew_mat = jnp.concatenate([phasor_im, -phasor_re], axis=2)
    real_part = jnp.einsum("pmk,qmk->pmq", left_mat, left_mat, preferred_element_type=jnp.float32)
    imag_part = jnp.einsum("pmk,qmk->pmq", skew_mat, left_mat, preferred_element_type=jnp.float32)
    packed_rows = lax.psum_scatter(
        (real_part + imag_part) * scaling, "dir", scatter_dimension=0, tiled=True
    )
    mirrored = lax.all_to_all(packed_rows, "dir", split_axis=2, concat_axis=0, tiled=True)
    mirrored = jnp.transpose(mirrored, (2, 1, 0))
    model_rows = jnp.stack([(packed_rows + mirrored) * 0.5, (packed_rows - mirrored) * 0.5], axis=2)
    row_ids = lax.axis_index("dir") * local_rows + jnp.arange(local_rows, dtype=jnp.int32)
    cross_baseline = (row_ids[:, None] != jnp.arange(stations, dtype=jnp.int32)[None, :]).astype(
        jnp.float32
    )
    baseline_keep = (
        jnp.tile(flags, (1, channels, 1)).astype(jnp.float32) * cross_baseline[:, None, :]
    )
    obs_rows = observed.reshape(local_rows, matrices, 2, stations)
    residual = baseline_keep[:, :, None, :] * (obs_rows - model_rows)
    resid_half = residual.astype(jnp.bfloat16)
    forward_mat = jnp.stack([left_mat, -skew_mat], axis=2)
    conj_mat = jnp.concatenate([phasor_re, -phasor_im], axis=2)
    dual_mat = jnp.concatenate([phasor_im, phasor_re], axis=2)
    adjoint_mat = jnp.stack([conj_mat, dual_mat], axis=2)
    rows_piece = lax.all_gather(resid_half, "dir", axis=0, tiled=True)
    row_part = jnp.einsum(
        "rmwq,qmwk->rmk", rows_piece, forward_mat, preferred_element_type=jnp.float32
    )
    col_total = jnp.einsum(
        "rmwp,rmwk->pmk", rows_piece, adjoint_mat, preferred_element_type=jnp.float32
    )
    weight_re = row_part[..., :local_sources] + col_total[..., :local_sources]
    weight_im = row_part[..., local_sources:] - col_total[..., local_sources:]
    source_grad = (
        phasor_im.astype(jnp.float32) * weight_re - phasor_re.astype(jnp.float32) * weight_im
    )
    source_grad = source_grad * (scaling / freq_each)[None, :, None]
    local_grad = jnp.einsum("pmk,kd->dp", source_grad, onehot_dirs, precision=highest)
    entry_count = local_dirs * dir_count * stations
    total_grad = lax.psum(local_grad, "freq")
    smooth = jnp.dot(total_grad, screen_kernel, precision=highest)
    total_sq = lax.psum(jnp.sum(smooth * smooth), "dir")
    updated = screen - step_size * smooth * lax.rsqrt(total_sq / entry_count + epsilon)
    return (residual.reshape(observed.shape), updated)


def solution(mesh):
    placed = (
        P("dir", "freq", None, None, None),
        P("dir", None, None),
        P("dir", None),
        P(),
        P(),
        P(None, "dir"),
        P("dir"),
        P("freq", None, None, None, "dir"),
        P("dir"),
        P("freq"),
    )
    return jax.shard_map(
        body,
        mesh=mesh,
        in_specs=placed,
        out_specs=(P("dir", "freq", None, None, None), P("dir", None)),
        check_vma=False,
    )
```

profile of v0, /device:TPU:0, one launch (start us, length us, event | category | flops | bytes accessed | tf_op | source)
XLA Modules:
  0.0 248.1 jit_solution(14236749292300200952)
XLA Ops:
  8.8 5.5 %copy.27 = f32[2,2,2,512,384]{3,4,1,0,2:T(8,128)} copy(bf16[2,2,2,512,384]{4,3,2,1,0:T(8,128)(2,1)} %param.17) | data formatting | bytes 9437184 | tf_op jit(solution)/shard_map/convert_element_type | solution.py:45
  14.9 14.2 %fusion.46 = (f32[512,4,384]{0,2,1:T(8,128)S(1)}, f32[512,4,384]{0,2,1:T(8,128)S(1)}) fusion(f32[4,2,512]{2,1,0:T(2,128)S(1)} %bitcast.86, f32[2,384]{1,0:T(2,128)S(1)} %copy-done.12, f32[4]{0:T(128)S(1)} %get-tuple-element.16, f32[4]{0:T(128)S(1)} %div.26, f32[512,384]{0,1:T(8,128)S(1)} %convolution_bitcast_fusion), kind=kOutput, calls=%fused_computation.68 | convolution fusion | flops 21233664 | bytes 7097376 | tf_op jit(solution)/shard_map/mcp,ck->pmk/dot_general | solution.py:40
  29.1 3.2 %fusion.45 = (bf16[512,4,384]{0,2,1:T(8,128)(2,1)}, bf16[512,4,384]{0,2,1:T(8,128)(2,1)S(1)}, bf16[512,4,1,384]{0,3,1,2:T(8,128)(2,1)}, bf16[512,4,384]{0,2,1:T(8,128)(2,1)S(1)}) fusion(f32[512,4,384]{0,2,1:T(8,128)S(1)} %get-tuple-element.10, f32[4,2,512,384]{2,3,0,1:T(8,128)S(1)} %bitcast.78, f32[512,4,384]{0,2,1:T(8,128)S(1)} %get-tuple-element.11, ...), kind=kLoop, calls=%fused_computation.67 | loop fusion | flops 9437184 | bytes 18875904 | tf_op jit(solution)/shard_map/neg | solution.py:74
  32.6 2.1 fusion.30
  34.7 3.5 %multiply_bitcast_fusion = f32[512,4,512]{0,2,1:T(8,128)} fusion(f32[4,512,512]{2,1,0:T(8,128)S(1)} %fusion.30, bf16[512,4,384]{0,2,1:T(8,128)(2,1)S(1)} %get-tuple-element.5, bf16[512,4,384]{0,2,1:T(8,128)(2,1)S(1)} %neg.16, bf16[512,4,384]{0,2,1:T(8,128)(2,1)S(1)} %get-tuple-element.7), kind=kOutput, calls=%fused_computation.8 | convolution fusion | flops 1625292800 | bytes 13107200 | tf_op jit(solution)/shard_map/pmk,qmk->pmq/dot_general | solution.py:56
  38.1 5.5 %copy.32 = f32[512,4,512]{2,1,0:T(4,128)} copy(f32[512,4,512]{0,2,1:T(8,128)} %multiply_bitcast_fusion) | data formatting | bytes 8388608 | tf_op jit(solution)/shard_map/mul | solution.py:58
  47.3 80.0 %all-reduce.3.cloned.1.call-done = f32[512,4,512]{2,1,0:T(4,128)} async-done(((f32[512,4,512]{2,1,0:T(4,128)}), f32[512,4,512]{2,1,0:T(4,128)}) %all-reduce.3.cloned.1.call-update) | async-done | bytes 4194320
  129.7 3.0 %reshape.106 = f32[8,1,16384]{2,1,0:T(1,128)} reshape(f32[512,4,64]{2,1,0:T(4,128)} %bitcast.83) | data formatting | bytes 1048576
  132.7 3.5 %all-to-all-start = ((f32[8,1,16384]{2,1,0:T(1,128)}), f32[8,1,16384]{2,1,0:T(1,128)S(1)}, u32[]{:S(2)}, u32[]{:S(2)}) async-start(f32[8,1,16384]{2,1,0:T(1,128)} %reshape.106), calls=%async_computation | async-start | bytes 1048576 | tf_op jit(solution)/shard_map/all_to_all | solution.py:60
  136.5 2.0 broadcast_multiply_fusion
  138.5 7.4 %all-to-all-done = f32[8,1,16384]{2,1,0:T(1,128)S(1)} async-done(((f32[8,1,16384]{2,1,0:T(1,128)}), f32[8,1,16384]{2,1,0:T(1,128)S(1)}, u32[]{:S(2)}, u32[]{:S(2)}) %all-to-all-start) | async-done | bytes 524320 | tf_op jit(solution)/shard_map/all_to_all | solution.py:60
  147.2 2.9 %reduce = f32[8,16384]{1,0:T(8,128)S(1)} reduce(f32[8,1,16384]{2,1,0:T(1,128)} %copy-done.7, f32[]{:T(128)} %broadcast.60), dimensions={1}, to_apply=%all_to_all.13.reduce_sub_computation | reduce | bytes 1048580 | tf_op jit(solution)/shard_map/all_to_all | solution.py:60
  151.8 2.8 %copy.64 = f32[64,4,8,64]{0,2,1,3:T(8,128)} copy(f32[64,4,8,64]{0,1,3,2:T(4,128)} %bitcast.84) | data formatting | bytes 1048576 | tf_op jit(solution)/shard_map/all_to_all | solution.py:60
  154.6 2.4 all_to_all.16
  162.0 4.4 %maximum_negate_fusion = bf16[512,4,1,768]{0,3,1,2:T(8,128)(2,1)} fusion(bf16[512,4,1,384]{0,3,1,2:T(8,128)(2,1)} %get-tuple-element.6, bf16[512,4,1,384]{0,3,1,2:T(8,128)(2,1)} %bitcast.79), kind=kLoop, calls=%fused_computation.29 | loop fusion | flops 7864320 | bytes 6291456 | tf_op jit(solution)/shard_map/neg | solution.py:73
  167.3 3.8 %fusion.29 = (bf16[512,4,1,768]{0,3,1,2:T(8,128)(2,1)}, bf16[512,4,1,768]{0,3,1,2:T(8,128)(2,1)}, bf16[512,4,1,768]{0,3,1,2:T(8,128)(2,1)}) fusion(bf16[512,4,384]{0,2,1:T(8,128)(2,1)S(1)} %copy-done.2, bf16[512,4,384]{0,2,1:T(8,128)(2,1)S(1)} %get-tuple-element.7, bf16[512,4,384]{0,2,1:T(8,128)(2,1)S(1)} %copy-done.4), kind=kLoop, calls=%fused_computation.34 | loop fusion | flops 17301504 | bytes 14155776 | tf_op jit(solution)/shard_map/stack | solution.py:73
  171.1 2.6 %stack.42 = f32[64,2,2,1,512]{4,3,2,1,0:T(1,128)} reshape(f32[64,4,512]{2,1,0:T(4,128)} %copy-done.5) | data formatting | bytes 1048576 | tf_op jit(solution)/shard_map/stack | solution.py:62
  175.2 3.9 %fusion.31 = f32[64,2,2,2,512]{4,3,2,1,0:T(2,128)} fusion(f32[64,2,2,2,512]{4,3,2,1,0:T(2,128)} %param.10, f32[64,2,2,1,512]{4,3,2,1,0:T(1,128)} %stack.43, f32[64,2,2,1,512]{4,3,2,1,0:T(1,128)} %stack.42, f32[64,2,2,512]{3,2,1,0:T(2,128)} %broadcast_multiply_fusion.1), kind=kLoop, calls=%fused_computation.38 | loop fusion | flops 786432 | bytes 3670016 | tf_op jit(solution)/shard_map/mul | solution.py:71
  179.1 18.7 %all-gather.2.cloned.1.call-done = bf16[512,4,2,512]{3,1,2,0:T(4,128)(2,1)} async-done(((bf16[64,4,2,512]{3,1,2,0:T(4,128)(2,1)}), bf16[512,4,2,512]{3,1,2,0:T(4,128)(2,1)}) %all-gather.2.cloned.1.call-update) | async-done | bytes 4194320 | tf_op jit(solution)/shard_map/all_gather | solution.py:77
  197.8 7.7 %fusion.24 = f32[512,4,768]{0,2,1:T(8,128)S(1)} fusion(bf16[512,4,2,512]{3,1,2,0:T(4,128)(2,1)} %all-gather.2.cloned.1.call-done, bf16[512,4,1,768]{0,3,1,2:T(8,128)(2,1)} %maximum_negate_fusion, bf16[512,4,1,768]{0,3,1,2:T(8,128)(2,1)} %get-tuple-element.8), kind=kOutput, calls=%fused_computation.33 | convolution fusion | flops 3224371200 | bytes 16777216 | tf_op jit(solution)/shard_map/rmwq,qmwk->rmk/dot_general | solution.py:78
  205.5 6.8 %fusion.19 = f32[512,4,768]{0,2,1:T(8,128)S(1)} fusion(bf16[512,4,2,512]{3,1,2,0:T(4,128)(2,1)} %all-gather.2.cloned.1.call-done, bf16[512,4,1,768]{0,3,1,2:T(8,128)(2,1)S(1)} %copy-done.6, bf16[512,4,1,768]{0,3,1,2:T(8,128)(2,1)} %get-tuple-element.12), kind=kOutput, calls=%fused_computation.32 | convolution fusion | flops 3224371200 | bytes 16777216 | tf_op jit(solution)/shard_map/rmwp,rmwk->pmk/dot_general | solution.py:81
  212.3 1.9 fusion.16
  214.7 11.7 %psum.14 = f32[2,512]{1,0:T(2,128)S(1)} all-reduce(f32[2,512]{1,0:T(2,128)S(1)} %fusion.36), channel_id=1, replica_groups=mesh['dir'=8,'freq'=4] {'freq'}, use_global_device_ids=true, to_apply=%region_2.0 | all-reduce | flops 1024 | bytes 8192 | tf_op jit(solution)/shard_map/psum | solution.py:92
  227.5 12.5 %psum.15 = f32[]{:T(128)} all-reduce(f32[]{:T(128)} %get-tuple-element.18), channel_id=1, replica_groups=mesh['dir'=8,'freq'=4] {'dir'}, use_global_device_ids=true, to_apply=%region_4.0 | all-reduce | flops 1 | bytes 8 | tf_op jit(solution)/shard_map/psum | solution.py:94
  (62 shorter events, 20.9 us)
Async XLA Ops:
  7.2 219.2 %copy-start = (f32[512,512]{1,0:T(8,128)S(1)}, f32[512,512]{1,0:T(8,128)}, u32[]{:S(2)}) copy-start(f32[512,512]{1,0:T(8,128)} %param.13) | copy-start | bytes 3145732
  7.2 120.1 %all-reduce.3.cloned.1.call-start = ((), (), s32[]{:S(2)}) async-start(), calls=%async_computation.2 | async-start | bytes 8388608
  8.8 5.5 %copy-start.9 = (f32[2,512]{1,0:T(2,128)S(1)}, f32[2,512]{1,0:T(2,128)}, u32[]{:S(2)}) copy-start(f32[2,512]{1,0:T(2,128)} %param.12) | copy-start | bytes 12292
  8.8 5.5 %copy-start.10 = (s32[384]{0:T(512)S(1)}, s32[384]{0:T(512)}, u32[]{:S(2)}) copy-start(s32[384]{0:T(512)} %param.18) | copy-start | bytes 4612
  8.8 6.0 %copy-start.11 = (f32[2,2,512]{2,1,0:T(2,128)S(1)}, f32[2,2,512]{2,1,0:T(2,128)}, u32[]{:S(2)}) copy-start(f32[2,2,512]{2,1,0:T(2,128)} %param.14) | copy-start | bytes 24580
  8.8 6.0 %copy-start.12 = (f32[2,384]{1,0:T(2,128)S(1)}, f32[2,384]{1,0:T(2,128)}, u32[]{:S(2)}) copy-start(f32[2,384]{1,0:T(2,128)} %param.15) | copy-start | bytes 9220
  14.8 14.2 %slice-start = ((s8[6291456]{0:T(1024)(128)(4,1)}), s8[4194304]{0:T(1024)(128)(4,1)S(1)}, s32[]{:S(2)}) async-start(s8[6291456]{0:T(1024)(128)(4,1)} %bitcast.76), calls=%async_computation.3 | async-start | bytes 8388608
  14.9 14.2 %slice-start.1 = ((s8[6291456]{0:T(1024)(128)(4,1)}), s8[2097152]{0:T(1024)(128)(4,1)S(1)}, s32[]{:S(2)}) async-start(s8[6291456]{0:T(1024)(128)(4,1)} %bitcast.76), calls=%async_computation.4 | async-start | bytes 4194304
  32.3 2.4 copy-start.1
  43.6 0.9 copy-start.8
  43.6 2.4 copy-start.13
  132.7 13.1 %all-to-all-start = ((f32[8,1,16384]{2,1,0:T(1,128)}), f32[8,1,16384]{2,1,0:T(1,128)S(1)}, u32[]{:S(2)}, u32[]{:S(2)}) async-start(f32[8,1,16384]{2,1,0:T(1,128)} %reshape.106), calls=%async_computation | async-start | bytes 1048576 | tf_op jit(solution)/shard_map/all_to_all | solution.py:60
  136.2 61.6 %all-gather.2.cloned.1.call-start = ((), (), s32[]{:S(2)}) async-start(), calls=%async_computation.1 | async-start | bytes 4718592 | tf_op jit(solution)/shard_map/all_gather | solution.py:77
  145.9 0.8 copy-start.7
  158.4 0.8 copy-start.5
  161.9 5.4 %copy-start.2 = (bf16[512,4,384]{0,2,1:T(8,128)(2,1)S(1)}, bf16[512,4,384]{0,2,1:T(8,128)(2,1)}, u32[]{:S(2)}) copy-start(bf16[512,4,384]{0,2,1:T(8,128)(2,1)} %copy-done.1) | copy-start | bytes 4718596
  162.0 5.4 %copy-start.4 = (bf16[512,4,384]{0,2,1:T(8,128)(2,1)S(1)}, bf16[512,4,384]{0,2,1:T(8,128)(2,1)}, u32[]{:S(2)}) copy-start(bf16[512,4,384]{0,2,1:T(8,128)(2,1)} %get-tuple-element.4) | copy-start | bytes 4718596
  197.8 7.8 %copy-start.6 = (bf16[512,4,1,768]{0,3,1,2:T(8,128)(2,1)S(1)}, bf16[512,4,1,768]{0,3,1,2:T(8,128)(2,1)}, u32[]{:S(2)}) copy-start(bf16[512,4,1,768]{0,3,1,2:T(8,128)(2,1)} %get-tuple-element.9) | copy-start | bytes 9437188
  205.5 6.8 %copy-start.3 = (bf16[512,4,384]{0,2,1:T(8,128)(2,1)S(1)}, bf16[512,4,384]{0,2,1:T(8,128)(2,1)}, u32[]{:S(2)}) copy-start(bf16[512,4,384]{0,2,1:T(8,128)(2,1)} %copy-done.1) | copy-start | bytes 4718596
Sparse Core Ops, SparseCore 0:
  43.8 83.5 all-reduce.2
  162.1 35.6 all-gather.1
where the time goes:
time: 249 us; the launch traced here: 248 us
  waiting for transfers between devices  106 us (43%)
  matrix products  36.4 us (15%)
  local copies, waits for them, and re-layouts  34.8 us (14%)
  other arithmetic  27.3 us (11%)
  blocking collectives  24.1 us (10%)
  between operations  15.6 us (6%)
  starting transfers between devices  3.75 us (2%)
    unnamed x3, waiting for transfers between devices  80.1 us
    all_gather x1, waiting for transfers between devices, body(): rows_piece = lax.all_gather(resid_half, 'dir', axis=0, tiled=True)  18.7 us
    dot_general x1, matrix products, body(): geometry = jnp.einsum('mcp,ck->pmk', uv_each, source_lm, precision=highest)  14.2 us
    psum x1, blocking collectives, body(): total_sq = lax.psum(jnp.sum(smooth * smooth), 'dir')  12.5 us
    psum x1, blocking collectives, body(): total_grad = lax.psum(local_grad, 'freq')  11.7 us
    unnamed x36, local copies, waits for them, and re-layouts  8.85 us
    dot_general x1, matrix products, body(): jnp.einsum('rmwq,qmwk->rmk', rows_piece, forward_mat, preferred_element_t...  7.74 us
    all_to_all x1, waiting for transfers between devices, body(): lax.all_to_all(packed_rows, 'dir', split_axis=2, concat_axis=0, tiled=True)  7.36 us
  transfers between devices with their start and end apart: 3, of which 3 were waited for; matrix products, arithmetic and copies ran while one was open for 9% of the time, Pallas kernels for 0%

commit v1 on v0

v1 whole, which is shorter than its diff:
```python
import functools
import math

import jax
import jax.numpy as jnp
from jax import lax
from jax.experimental import pallas as pl
from jax.experimental.pallas import tpu as pltpu
from jax.sharding import PartitionSpec as P

step_size = 0.3
epsilon = 1e-06
MESH = pl.DeviceIdType.MESH
f32 = jnp.float32
bf16 = jnp.bfloat16

SIN_POLY = (6.283185272722381, -41.341697068949564, 81.60502462236155, -76.70155117323625, 42.01616580115987, -14.868610927638132, 3.19969357384433)
COS_POLY = (0.9999999891722522, -19.739204532086525, 64.93911898351571, -85.45016554378464, 60.16783168053616, -25.968313120273056, 6.5296101719799085)


def horner(coefs, z):
    total = jnp.full_like(z, coefs[-1])
    for c in coefs[-2::-1]:
        total = total * z + c
    return total


def kernel(
    n_dir,
    n_freq,
    scaling,
    ratio_ref,
    gain_hbm,
    cols_ref,
    src_ref,
    dirs_ref,
    kobs_hbm,
    keep_hbm,
    screen_ref,
    kern_hbm,
    own_ref,
    mirror_ref,
    updated_ref,
    gain,
    kobs,
    keep,
    kern,
    left,
    mixed,
    pfull,
    pdir,
    s1buf,
    r1buf,
    s2buf,
    qown,
    r2buf,
    ugath,
    rowacc,
    colacc,
    gbuf,
    sqbuf,
    tbuf,
    gain_sem,
    in_sem,
    s1_send,
    s1_recv,
    s2_send,
    s2_recv,
    ag_send,
    ag_recv,
    fw_send,
    fr_send,
    fr_recv,
    sq_send,
    sq_recv,
):
    count, _, stations, sources = gain.shape
    local_dirs = pdir.shape[0]
    times = keep.shape[0]
    rows = kobs.shape[1]
    chips = n_dir // 2
    me = lax.axis_index("dir")
    fme = lax.axis_index("freq")
    core = lax.rem(me, 2)
    chip = lax.div(me, 2)
    partner = chip * 2 + 1 - core

    def gain_copy(m):
        return pltpu.make_async_copy(gain_hbm.at[m], gain.at[m], gain_sem.at[m])

    for m in range(count):
        gain_copy(m).start()
    in_copies = [
        pltpu.make_async_copy(kobs_hbm, kobs, in_sem.at[0]),
        pltpu.make_async_copy(keep_hbm, keep, in_sem.at[1]),
        pltpu.make_async_copy(kern_hbm, kern, in_sem.at[2]),
    ]
    for c in in_copies:
        c.start()

    barrier = pltpu.get_barrier_semaphore()
    for o in range(1, n_dir):
        pl.semaphore_signal(
            barrier, inc=1, device_id={"dir": lax.rem(me + o, n_dir)}, device_id_type=MESH
        )
    for o in range(1, n_freq):
        pl.semaphore_signal(
            barrier, inc=1, device_id={"freq": lax.rem(fme + o, n_freq)}, device_id_type=MESH
        )

    rowacc[...] = jnp.zeros_like(rowacc)
    colacc[...] = jnp.zeros_like(colacc)

    def remote(src, dst, send, recv, axis, where):
        return pltpu.make_async_remote_copy(
            src_ref=src,
            dst_ref=dst,
            send_sem=send,
            recv_sem=recv,
            device_id={axis: where},
            device_id_type=MESH,
        )

    def s1_copy(m):
        return remote(s1buf.at[m], r1buf.at[m], s1_send.at[m], s1_recv.at[m], "dir", partner)

    def s2_copy(m, o):
        to = lax.rem(chip + o, chips)
        return remote(
            s2buf.at[m, to],
            r2buf.at[m, o],
            s2_send.at[m, o],
            s2_recv.at[m, o],
            "dir",
            to * 2 + core,
        )

    def row_slice(owner):
        return pl.ds(pl.multiple_of(owner * rows, rows), rows)

    def ag_copy(m, o):
        to = partner if o == 0 else lax.rem(chip + o, chips) * 2 + core
        piece = ugath.at[m, row_slice(me), :]
        return remote(piece, piece, ag_send.at[m, o], ag_recv.at[m, o], "dir", to)

    def fw_copy(m, o):
        owner = lax.rem(chip - o + chips, chips) * 2 + core
        piece = ugath.at[m, row_slice(owner), :]
        return remote(piece, piece, fw_send.at[m, o], ag_recv.at[m, chips + o - 1], "dir", partner)

    chunk = 32

    def phasors(m):
        gain_copy(m).wait()

        def one(i, _):
            at = pl.ds(pl.multiple_of(i * chunk, chunk), chunk)
            col = cols_ref[m, at, :]
            lm = src_ref[...]
            turns = col[:, 0:1] * lm[0:1] + col[:, 1:2] * lm[1:2]
            own = jnp.broadcast_to(col[:, 2:3], turns.shape)
            for d in range(1, local_dirs):
                own = jnp.where(dirs_ref[0:1, :] == d, col[:, 2 + d : 3 + d], own)
            turns = turns + own
            r = turns - jnp.round(turns)
            z = r * r
            amp = lm[2:3]
            sine = horner(SIN_POLY, z) * (r * amp)
            cosine = horner(COS_POLY, z) * amp
            g_re = gain[m, 0, at, :].astype(f32)
            g_im = gain[m, 1, at, :].astype(f32)
            re = (g_re * cosine - g_im * sine).astype(bf16)
            im = (g_re * sine + g_im * cosine).astype(bf16)
            left[m, at, :sources] = re
            left[m, at, sources:] = im
            re = re.astype(f32)
            im = im.astype(f32)
            mixed[m, at, :sources] = (re + im).astype(bf16)
            mixed[m, at, sources:] = (im - re).astype(bf16)
            return 0

        lax.fori_loop(0, stations // chunk, one, 0)

    def nt_dot(a, b):
        return lax.dot_general(a, b, (((1,), (1,)), ((), ())), preferred_element_type=f32)

    def partial_model(m):
        pfull[m] = nt_dot(mixed[m], left[m]).reshape(chips, 2, rows, stations)

        def one(j, _):
            s1buf[m, j] = pfull[m, j, 1 - core].astype(bf16)
            return 0

        lax.fori_loop(0, chips, one, 0)

    def chip_sum(m):
        s1_copy(m).wait_recv()

        def one(j, _):
            total = pfull[m, j, core] + r1buf[m, j].astype(f32)
            s2buf[m, j] = total.astype(bf16)
            return 0

        lax.fori_loop(0, chips, one, 0)
        for o in range(1, chips):
            s2_copy(m, o).start()
        qown[m] = pfull[m, chip, core] + r1buf[m, chip].astype(f32)

    def own_residual(m):
        total = qown[m]
        for o in range(1, chips):
            s2_copy(m, o).wait_recv()
            total = total + r2buf[m, o].astype(f32)
        value = kobs[m] - keep[lax.rem(m, times)] * (total * scaling)
        own_ref[m] = value
        ugath[m, row_slice(me), :] = value.astype(bf16)
        for o in list(range(1, chips)) + [0]:
            ag_copy(m, o).start()

    def forward(m):
        for o in range(1, chips):
            ag_copy(m, o).wait_recv()
            fw_copy(m, o).start()

    def direction_models(m):
        for d in range(local_dirs):
            mask = jnp.where(dirs_ref[...] == d, 1.0, 0.0).astype(bf16)
            mask = jnp.concatenate([mask, mask], axis=1)[0:1]
            pdir[d] = nt_dot(left[m] * mask, mixed[m])

    def local_grad(m):
        ag_copy(m, 0).wait_recv()
        for o in range(1, chips):
            fw_copy(m, o).wait_recv()
        weight = scaling / ratio_ref[0, lax.div(m, times)]

        def one(i, carry):
            at = pl.ds(pl.multiple_of(i * chunk, chunk), chunk)
            u = ugath[m, at, :].astype(f32) * weight
            out = []
            for d in range(local_dirs):
                w = u * pdir[d, at, :]
                part = w[:, 0:128]
                for b in range(1, stations // 128):
                    part = part + w[:, b * 128 : (b + 1) * 128]
                rowacc[d, at, :] += part
                c = carry[d]
                for b in range(chunk // 8):
                    c = c + w[b * 8 : (b + 1) * 8]
                out.append(c)
            return tuple(out)

        init = tuple(colacc[d] for d in range(local_dirs))
        out = lax.fori_loop(0, stations // chunk, one, init)
        for d in range(local_dirs):
            colacc[d] = out[d]

    def step(s, _):
        @pl.when(s < count)
        def _():
            phasors(s)
            partial_model(s)

            @pl.when(s == 0)
            def _():
                pl.semaphore_wait(barrier, n_dir - 1 + n_freq - 1)
                for c in in_copies:
                    c.wait()

            s1_copy(s).start()

        @pl.when(jnp.logical_and(s >= 1, s < count + 1))
        def _():
            chip_sum(s - 1)

        @pl.when(jnp.logical_and(s >= 2, s < count + 2))
        def _():
            own_residual(s - 2)

        @pl.when(jnp.logical_and(s >= 3, s < count + 3))
        def _():
            forward(s - 3)

        @pl.when(s >= 4)
        def _():
            local_grad(s - 4)

        @pl.when(jnp.logical_and(s >= 3, s < count + 3))
        def _():
            direction_models(s - 3)

        return 0

    lax.fori_loop(0, count + 4, step, 0)

    mine = []
    for d in range(local_dirs):
        by_col = jnp.sum(colacc[d], axis=0, keepdims=True)
        by_row = jnp.sum(jnp.transpose(rowacc[d]), axis=0, keepdims=True)
        mine.append(by_col - by_row)
    mine.append(jnp.zeros((8 - local_dirs, stations), f32))
    gbuf[fme] = jnp.concatenate(mine, axis=0)

    def fr_copy(o):
        slot = gbuf.at[fme]
        return remote(
            slot, slot, fr_send.at[o], fr_recv.at[o], "freq", lax.rem(fme + o, n_freq)
        )

    for o in range(1, n_freq):
        fr_copy(o).start()

    group = 128 // rows
    lane0 = pl.multiple_of(lax.div(me, group) * 128, 128)
    sub0 = pl.multiple_of(lax.rem(me, group) * rows, rows)

    def mirror(m, _):
        for b in range(stations // 128):
            block = ugath[m, b * 128 : (b + 1) * 128, pl.ds(lane0, 128)].astype(f32)
            tbuf[:, b * 128 : (b + 1) * 128] = jnp.transpose(block)
        mirror_ref[m] = tbuf[pl.ds(sub0, rows), :]
        return 0

    lax.fori_loop(0, count, mirror, 0)

    for o in range(1, n_freq):
        fr_copy(o).wait_recv()
    total = gbuf[0]
    for f in range(1, n_freq):
        total = total + gbuf[f]
    smooth = jnp.dot(
        total, kern[...], preferred_element_type=f32, precision=lax.Precision.HIGHEST
    )
    squares = smooth * smooth
    part = squares[:, 0:128]
    for b in range(1, stations // 128):
        part = part + squares[:, b * 128 : (b + 1) * 128]
    sqbuf[0] = part

    def sq_copy(o):
        return remote(
            sqbuf.at[0], sqbuf.at[o], sq_send.at[o], sq_recv.at[o], "dir", lax.rem(me + o, n_dir)
        )

    for o in range(1, n_dir):
        sq_copy(o).start()
    for o in range(1, n_dir):
        sq_copy(o).wait_recv()
        part = part + sqbuf[o]
    total_sq = jnp.sum(jnp.sum(part, axis=1, keepdims=True), axis=0, keepdims=True)
    scale = step_size * lax.rsqrt(total_sq / (local_dirs * n_dir * stations) + epsilon)
    updated_ref[...] = screen_ref[...] - smooth[:local_dirs] * scale

    def drain(m, _):
        s1_copy(m).wait_send()
        for o in range(1, chips):
            s2_copy(m, o).wait_send()
            fw_copy(m, o).wait_send()
        for o in range(chips):
            ag_copy(m, o).wait_send()
        return 0

    lax.fori_loop(0, count, drain, 0)
    for o in range(1, n_freq):
        fr_copy(o).wait_send()
    for o in range(1, n_dir):
        sq_copy(o).wait_send()


def body(
    observed,
    flags,
    screen,
    screen_kernel,
    station_uv,
    source_lm,
    source_flux,
    station_gain,
    source_direction,
    freq_ratio,
):
    n_dir = lax.axis_size("dir")
    n_freq = lax.axis_size("freq")
    local_dirs, stations = screen.shape
    sources = source_flux.shape[0]
    rows = observed.shape[0]
    channels = freq_ratio.shape[0]
    times = station_uv.shape[0]
    count = channels * times
    chips = n_dir // 2
    scaling = 1.0 / math.sqrt(sources * n_dir)

    gain = station_gain.reshape(count, 2, stations, sources)
    freq_each = jnp.repeat(freq_ratio, times)
    uv = jnp.tile(station_uv, (channels, 1, 1)) * freq_each[:, None, None]
    screens = screen[None] / (freq_each * (2.0 * math.pi))[:, None, None]
    cols = jnp.concatenate([uv, screens], axis=1)
    cols = jnp.pad(cols, ((0, 0), (0, 8 - cols.shape[1]), (0, 0)))
    cols = jnp.transpose(cols, (0, 2, 1))
    src = jnp.concatenate([source_lm, jnp.sqrt(source_flux)[None]], axis=0)
    src = jnp.pad(src, ((0, 8 - src.shape[0]), (0, 0)))
    dirs = jnp.broadcast_to(source_direction[None], (8, sources))

    row_ids = lax.axis_index("dir") * rows + jnp.arange(rows, dtype=jnp.int32)
    cross = row_ids[:, None] != jnp.arange(stations, dtype=jnp.int32)[None, :]
    keep = jnp.transpose(flags, (1, 0, 2)).astype(f32) * cross.astype(f32)[None]
    packed = (observed[:, :, :, 0] + observed[:, :, :, 1]).reshape(rows, count, stations)
    kobs = jnp.transpose(packed, (1, 0, 2)) * jnp.tile(keep, (channels, 1, 1))

    vmem = pl.BlockSpec(memory_space=pltpu.VMEM)
    hbm = pl.BlockSpec(memory_space=pl.ANY)
    dma = pltpu.SemaphoreType.DMA
    own, mirrored, updated = pl.pallas_call(
        functools.partial(kernel, n_dir, n_freq, scaling),
        out_shape=(
            jax.ShapeDtypeStruct((count, rows, stations), f32),
            jax.ShapeDtypeStruct((count, rows, stations), f32),
            jax.ShapeDtypeStruct((local_dirs, stations), f32),
        ),
        in_specs=[
            pl.BlockSpec(memory_space=pltpu.SMEM),
            hbm,
            vmem,
            vmem,
            vmem,
            hbm,
            hbm,
            vmem,
            hbm,
        ],
        out_specs=(vmem, vmem, vmem),
        scratch_shapes=[
            pltpu.VMEM((count, 2, stations, sources), bf16),
            pltpu.VMEM((count, rows, stations), f32),
            pltpu.VMEM((times, rows, stations), f32),
            pltpu.VMEM((stations, stations), f32),
            pltpu.VMEM((count, stations, 2 * sources), bf16),
            pltpu.VMEM((count, stations, 2 * sources), bf16),
            pltpu.VMEM((count, chips, 2, rows, stations), f32),
            pltpu.VMEM((local_dirs, stations, stations), f32),
            pltpu.VMEM((count, chips, rows, stations), bf16),
            pltpu.VMEM((count, chips, rows, stations), bf16),
            pltpu.VMEM((count, chips, rows, stations), bf16),
            pltpu.VMEM((count, rows, stations), f32),
            pltpu.VMEM((count, chips, rows, stations), bf16),
            pltpu.VMEM((count, stations, stations), bf16),
            pltpu.VMEM((local_dirs, stations, 128), f32),
            pltpu.VMEM((local_dirs, 8, stations), f32),
            pltpu.VMEM((n_freq, 8, stations), f32),
            pltpu.VMEM((n_dir, 8, 128), f32),
            pltpu.VMEM((128, stations), f32),
            dma((count,)),
            dma((3,)),
            dma((count,)),
            dma((count,)),
            dma((count, chips)),
            dma((count, chips)),
            dma((count, chips)),
            dma((count, 2 * chips)),
            dma((count, chips)),
            dma((n_freq,)),
            dma((n_freq,)),
            dma((n_dir,)),
            dma((n_dir,)),
        ],
        compiler_params=pltpu.CompilerParams(
            collective_id=0, has_side_effects=True, vmem_limit_bytes=60 * 1024 * 1024
        ),
        name="calibrate",
    )(
        freq_ratio[None],
        gain,
        cols,
        src,
        dirs,
        kobs,
        keep,
        screen,
        screen_kernel,
    )
    residual = jnp.stack([(own + mirrored) * 0.5, (own - mirrored) * 0.5], axis=1)
    residual = jnp.transpose(residual, (2, 0, 1, 3))
    return (residual.reshape(observed.shape), updated)


def solution(mesh):
    placed = (
        P("dir", "freq", None, None, None),
        P("dir", None, None),
        P("dir", None),
        P(),
        P(),
        P(None, "dir"),
        P("dir"),
        P("freq", None, None, None, "dir"),
        P("dir"),
        P("freq"),
    )
    return jax.shard_map(
        body,
        mesh=mesh,
        in_specs=placed,
        out_specs=(P("dir", "freq", None, None, None), P("dir", None)),
        check_vma=False,
    )
```

time: 249 us -> 65.6 us (0.26)
  waiting for transfers between devices: 106 us -> 0 us
  Pallas kernels: 0 us -> 49.6 us
  matrix products: 36.4 us -> 0 us
  local copies, waits for them, and re-layouts: 34.8 us -> 6.74 us
  blocking collectives: 24.1 us -> 0 us
  other arithmetic: 27.3 us -> 8.16 us
  between operations: 15.6 us -> 0.73 us
  starting transfers between devices: 3.75 us -> 0 us
    unnamed x3 -> x0, waiting for transfers between devices: 80.1 us -> none
    pallas_call x0 -> x1, Pallas kernels: none -> 49.6 us  [body(): pl.pallas_call(functools.partial(kernel, n_dir, n_freq, scaling), out_sha...]
    dot_general x8 -> x0, matrix products: 36.4 us -> none  [the longest x1 14.2 us: body(): geometry = jnp.einsum('mcp,ck->pmk', uv_each, source_lm, precision=highest)]
    psum x2 -> x0, blocking collectives: 24.1 us -> none  [the longest x1 12.5 us: body(): total_sq = lax.psum(jnp.sum(smooth * smooth), 'dir')]
    all_gather x1 -> x0, waiting for transfers between devices: 18.7 us -> none  [body(): rows_piece = lax.all_gather(resid_half, 'dir', axis=0, tiled=True)]
    neg x3 -> x0, other arithmetic: 7.88 us -> none  [the longest x1 4.38 us: body(): forward_mat = jnp.stack([left_mat, -skew_mat], axis=2)]
    convert_element_type x3 -> x0, local copies, waits for them, and re-layouts: 7.68 us -> none  [the longest x1 5.46 us: body(): station_gain.reshape(matrices, 2, stations, local_sources)]
    all_to_all x1 -> x0, waiting for transfers between devices: 7.36 us -> none  [body(): lax.all_to_all(packed_rows, 'dir', split_axis=2, concat_axis=0, tiled=True)]
  transfers between devices with their start and end apart: 3 -> 0, of which waited for: 3 -> 0; matrix products, arithmetic and copies ran while one was open for 9% -> 0% of each run, Pallas kernels for 0% -> 0%
where the time goes in v1:
time: 65.6 us; the launch traced here: 65.3 us
  Pallas kernels  49.6 us (76%)
  other arithmetic  8.16 us (12%)
  local copies, waits for them, and re-layouts  6.74 us (10%)
  between operations  0.73 us (1%)
    pallas_call x1, Pallas kernels, body(): pl.pallas_call(functools.partial(kernel, n_dir, n_freq, scaling), out_sha...  49.6 us
    add x1, other arithmetic, body(): observed[:, :, :, 0] + observed[:, :, :, 1]  2.63 us
    unnamed x6, local copies, waits for them, and re-layouts  2.38 us
    another operation x2, other arithmetic, body(): jnp.stack([(own + mirrored) * 0.5, (own - mirrored) * 0.5], axis=1)  1.47 us

profile of v1, /device:TPU:0, one launch (start us, length us, event | category | flops | bytes accessed | tf_op | source)
XLA Modules:
  0.0 65.3 jit_solution(7894397269954170628)
XLA Ops:
  0.6 0.7 %broadcast_in_dim.9 = f32[2,2]{1,0:T(2,128)S(1)} broadcast(f32[2]{0:T(128)} %param.19), dimensions={0} | broadcast | bytes 24 | tf_op jit(solution)/shard_map/broadcast_in_dim | solution.py:394
  1.4 0.1 mul.39
  1.5 0.7 %sqrt.3 = f32[384]{0:T(512)S(1)} sqrt(f32[384]{0:T(512)} %param.16) | non-fusion elementwise | bytes 3072 | tf_op jit(solution)/shard_map/sqrt | solution.py:400
  2.2 1.3 %select_maximum_fusion.src_ref = f32[8,384]{1,0:T(8,128)} fusion(f32[1,384]{1,0:T(1,128)S(1)} %broadcast_in_dim.10, f32[2,384]{1,0:T(2,128)} %param.15), kind=kLoop, calls=%fused_computation.13 | loop fusion | flops 12288 | bytes 16896 | tf_op jit(solution)/shard_map/concatenate | solution.py:400
  3.4 1.3 %broadcast_in_dim.11.dirs_ref = s32[8,384]{1,0:T(8,128)} broadcast(s32[384]{0:T(512)} %param.18), dimensions={1} | broadcast | bytes 13824 | tf_op jit(solution)/shard_map/broadcast_in_dim | solution.py:402
  4.7 0.8 %bitcast_multiply_fusion.1 = (f32[4,2,512]{2,1,0:T(2,128)S(1)}, f32[4,2,512]{2,1,0:T(2,128)S(1)}) fusion(f32[4]{0:T(128)S(1)} %mul.39, f32[2,2,512]{2,1,0:T(2,128)} %param.14, f32[4]{0:T(128)S(1)} %broadcast_multiply_fusion, f32[2,512]{1,0:T(2,128)} %screen_ref.1), kind=kLoop, calls=%fused_computation.12 | loop fusion | flops 8192 | bytes 45088 | tf_op jit(solution)/shard_map/mul | solution.py:395
  5.5 0.1 fusion.2
  5.6 1.0 %fusion.1.keep_hbm = f32[2,64,512]{2,1,0:T(8,128)S(1)} fusion(s32[64,2,512]{2,1,0:T(2,128)} %param.11, f32[64,512]{1,0:T(8,128)S(1)} %fusion.2), kind=kLoop, calls=%fused_computation.8 | loop fusion | flops 131072 | bytes 655360 | tf_op jit(solution)/shard_map/mul | solution.py:406
  6.6 0.0 copy-start
  6.6 2.6 %slice_add_fusion = f32[64,2,2,1,512]{4,3,2,1,0:T(1,128)S(1)} fusion(f32[64,2,2,2,512]{4,3,2,1,0:T(2,128)} %param.10), kind=kLoop, calls=%fused_computation.5 | loop fusion | flops 131072 | bytes 1572864 | tf_op jit(solution)/shard_map/add | solution.py:407
  9.3 0.2 copy.18
  9.5 0.9 %bitcast_multiply_fusion.kobs_hbm = f32[4,64,512]{2,1,0:T(8,128)} fusion(f32[64,2,2,1,512]{4,0,2,1,3:T(8,128)S(1)} %copy.18, f32[2,64,512]{2,1,0:T(8,128)S(1)} %fusion.1.keep_hbm), kind=kLoop, calls=%fused_computation.2 | loop fusion | flops 131072 | bytes 1310720 | tf_op jit(solution)/shard_map/mul | solution.py:408
  10.3 0.4 copy.17
  10.7 1.0 %pad_bitcast_fusion.cols_ref = f32[4,512,8]{2,1,0:T(8,128)} fusion(f32[4,4,512]{1,2,0:T(8,128)S(1)} %copy.17), kind=kLoop, calls=%fused_computation.1 | loop fusion | bytes 98304 | tf_op jit(solution)/shard_map/transpose | solution.py:399
  11.7 0.0 copy-done
  11.7 49.6 %calibrate.1 = (f32[4,64,512]{2,1,0:T(8,128)}, f32[4,64,512]{2,1,0:T(8,128)}, f32[2,512]{1,0:T(2,128)}) custom-call(f32[1,2]{1,0:T(1,128)} %bitcast.23, bf16[4,2,512,384]{3,2,1,0:T(8,128)(2,1)} %bitcast.22, f32[4,512,8]{2,1,0:T(8,128)} %pad_bitcast_fusion.cols_ref, f32[8,384]{1,0:T(8,128)} %select_maximum_fusion.src_ref, ...), custom_call_target="tpu_custom_call" | custom-call | tf_op jit(solution)/shard_map/calibrate/pallas_call | solution.py:413
  61.4 0.0 copy-start.1
  61.4 1.4 %multiply_bitcast_fusion.1 = (f32[4,1,64,512]{3,2,0,1:T(8,128)S(1)}, f32[4,1,64,512]{3,2,0,1:T(8,128)S(1)}) fusion(f32[4,64,512]{2,1,0:T(8,128)} %get-tuple-element.5, f32[4,64,512]{2,1,0:T(8,128)} %get-tuple-element.6), kind=kLoop, calls=%fused_computation.4 | loop fusion | flops 524288 | bytes 2097152 | tf_op jit(solution)/shard_map/stack | solution.py:481
  62.8 0.1 pad_maximum_fusion
  62.9 1.8 %copy.20 = f32[64,2,2,2,512]{4,3,2,1,0:T(2,128)} copy(f32[64,2,2,2,512]{4,0,2,1,3:T(8,128)S(1)} %bitcast.21) | data formatting | bytes 2097152
  64.7 0.0 copy-done.1
  64.7 0.6 copy.27
  (4 shorter events, 0.0 us)
Async XLA Ops:
  6.6 5.1 %copy-start = (f32[2,64,512]{2,1,0:T(8,128)}, f32[2,64,512]{2,1,0:T(8,128)S(1)}, u32[]{:S(2)}) copy-start(f32[2,64,512]{2,1,0:T(8,128)S(1)} %fusion.1.keep_hbm) | copy-start | bytes 786436
  61.4 3.3 %copy-start.1 = (f32[2,512]{1,0:T(2,128)S(1)}, f32[2,512]{1,0:T(2,128)}, u32[]{:S(2)}) copy-start(f32[2,512]{1,0:T(2,128)} %get-tuple-element.19) | copy-start | bytes 12292

commit v2 on v1

--- a/solution.py
+++ b/solution.py
@@ -31,20 +31,22 @@
     scaling,
     ratio_ref,
     gain_hbm,
-    cols_ref,
-    src_ref,
+    uv_ref,
+    lm_ref,
+    flux_ref,
     dirs_ref,
-    kobs_hbm,
-    keep_hbm,
+    obs_hbm,
+    flags_hbm,
     screen_ref,
     kern_hbm,
-    own_ref,
-    mirror_ref,
+    resid_ref,
     updated_ref,
     gain,
-    kobs,
-    keep,
+    obs,
+    flags,
     kern,
+    cols,
+    own_res,
     left,
     mixed,
     pfull,
@@ -76,8 +78,9 @@
 ):
     count, _, stations, sources = gain.shape
     local_dirs = pdir.shape[0]
-    times = keep.shape[0]
-    rows = kobs.shape[1]
+    times = uv_ref.shape[0]
+    rows = own_res.shape[1]
+    tiles = stations // 128
     chips = n_dir // 2
     me = lax.axis_index("dir")
     fme = lax.axis_index("freq")
@@ -91,8 +94,8 @@
     for m in range(count):
         gain_copy(m).start()
     in_copies = [
-        pltpu.make_async_copy(kobs_hbm, kobs, in_sem.at[0]),
-        pltpu.make_async_copy(keep_hbm, keep, in_sem.at[1]),
+        pltpu.make_async_copy(obs_hbm, obs, in_sem.at[0]),
+        pltpu.make_async_copy(flags_hbm, flags, in_sem.at[1]),
         pltpu.make_async_copy(kern_hbm, kern, in_sem.at[2]),
     ]
     for c in in_copies:
@@ -108,6 +111,11 @@
             barrier, inc=1, device_id={"freq": lax.rem(fme + o, n_freq)}, device_id_type=MESH
         )
 
+    for m in range(count):
+        ratio = ratio_ref[0, m // times]
+        parts = [uv_ref[m % times] * ratio, screen_ref[...] / (ratio * (2.0 * math.pi))]
+        parts.append(jnp.zeros((8 - 2 - local_dirs, stations), f32))
+        cols[m] = jnp.transpose(jnp.concatenate(parts, axis=0))
     rowacc[...] = jnp.zeros_like(rowacc)
     colacc[...] = jnp.zeros_like(colacc)
 
@@ -155,16 +163,16 @@
 
         def one(i, _):
             at = pl.ds(pl.multiple_of(i * chunk, chunk), chunk)
-            col = cols_ref[m, at, :]
-            lm = src_ref[...]
+            col = cols[m, at, :]
+            lm = lm_ref[...]
             turns = col[:, 0:1] * lm[0:1] + col[:, 1:2] * lm[1:2]
             own = jnp.broadcast_to(col[:, 2:3], turns.shape)
             for d in range(1, local_dirs):
-                own = jnp.where(dirs_ref[0:1, :] == d, col[:, 2 + d : 3 + d], own)
+                own = jnp.where(dirs_ref[...] == d, col[:, 2 + d : 3 + d], own)
             turns = turns + own
             r = turns - jnp.round(turns)
             z = r * r
-            amp = lm[2:3]
+            amp = jnp.sqrt(flux_ref[...])
             sine = horner(SIN_POLY, z) * (r * amp)
             cosine = horner(COS_POLY, z) * amp
             g_re = gain[m, 0, at, :].astype(f32)
@@ -211,9 +219,18 @@
         for o in range(1, chips):
             s2_copy(m, o).wait_recv()
             total = total + r2buf[m, o].astype(f32)
-        value = kobs[m] - keep[lax.rem(m, times)] * (total * scaling)
-        own_ref[m] = value
-        ugath[m, row_slice(me), :] = value.astype(bf16)
+        row_ids = me * rows + lax.broadcasted_iota(jnp.int32, (rows, 128), 0)
+        lane_ids = lax.broadcasted_iota(jnp.int32, (rows, 128), 1)
+        for b in range(tiles):
+            lanes = slice(b * 128, (b + 1) * 128)
+            at = (m * tiles + b) * 2
+            real = obs[pl.ds(at, rows, stride=count * tiles * 2), :]
+            imag = obs[pl.ds(at + 1, rows, stride=count * tiles * 2), :]
+            flag = flags[pl.ds(b * times + lax.rem(m, times), rows, stride=tiles * times), :]
+            keep = jnp.where(row_ids == lane_ids + b * 128, 0, flag).astype(f32)
+            value = keep * (real + imag - total[:, lanes] * scaling)
+            own_res[m, :, lanes] = value
+            ugath[m, row_slice(me), lanes] = value.astype(bf16)
         for o in list(range(1, chips)) + [0]:
             ag_copy(m, o).start()
 
@@ -225,7 +242,7 @@
     def direction_models(m):
         for d in range(local_dirs):
             mask = jnp.where(dirs_ref[...] == d, 1.0, 0.0).astype(bf16)
-            mask = jnp.concatenate([mask, mask], axis=1)[0:1]
+            mask = jnp.concatenate([mask, mask], axis=1)
             pdir[d] = nt_dot(left[m] * mask, mixed[m])
 
     def local_grad(m):
@@ -314,14 +331,15 @@
     lane0 = pl.multiple_of(lax.div(me, group) * 128, 128)
     sub0 = pl.multiple_of(lax.rem(me, group) * rows, rows)
 
-    def mirror(m, _):
-        for b in range(stations // 128):
+    for m in range(count):
+        for b in range(tiles):
             block = ugath[m, b * 128 : (b + 1) * 128, pl.ds(lane0, 128)].astype(f32)
-            tbuf[:, b * 128 : (b + 1) * 128] = jnp.transpose(block)
-        mirror_ref[m] = tbuf[pl.ds(sub0, rows), :]
-        return 0
-
-    lax.fori_loop(0, count, mirror, 0)
+            tbuf[m, b] = jnp.transpose(block)
+            turned = tbuf[m, b, pl.ds(sub0, rows), :]
+            own = own_res[m, :, b * 128 : (b + 1) * 128]
+            at = (m * tiles + b) * 2
+            resid_ref[pl.ds(at, rows, stride=count * tiles * 2), :] = (own + turned) * 0.5
+            resid_ref[pl.ds(at + 1, rows, stride=count * tiles * 2), :] = (own - turned) * 0.5
 
     for o in range(1, n_freq):
         fr_copy(o).wait_recv()
@@ -390,31 +408,20 @@
     chips = n_dir // 2
     scaling = 1.0 / math.sqrt(sources * n_dir)
 
+    tiles = stations // 128
     gain = station_gain.reshape(count, 2, stations, sources)
-    freq_each = jnp.repeat(freq_ratio, times)
-    uv = jnp.tile(station_uv, (channels, 1, 1)) * freq_each[:, None, None]
-    screens = screen[None] / (freq_each * (2.0 * math.pi))[:, None, None]
-    cols = jnp.concatenate([uv, screens], axis=1)
-    cols = jnp.pad(cols, ((0, 0), (0, 8 - cols.shape[1]), (0, 0)))
-    cols = jnp.transpose(cols, (0, 2, 1))
-    src = jnp.concatenate([source_lm, jnp.sqrt(source_flux)[None]], axis=0)
-    src = jnp.pad(src, ((0, 8 - src.shape[0]), (0, 0)))
-    dirs = jnp.broadcast_to(source_direction[None], (8, sources))
-
-    row_ids = lax.axis_index("dir") * rows + jnp.arange(rows, dtype=jnp.int32)
-    cross = row_ids[:, None] != jnp.arange(stations, dtype=jnp.int32)[None, :]
-    keep = jnp.transpose(flags, (1, 0, 2)).astype(f32) * cross.astype(f32)[None]
-    packed = (observed[:, :, :, 0] + observed[:, :, :, 1]).reshape(rows, count, stations)
-    kobs = jnp.transpose(packed, (1, 0, 2)) * jnp.tile(keep, (channels, 1, 1))
+    obs = observed.reshape(rows, count, 2, tiles, 128)
+    obs = jnp.transpose(obs, (0, 1, 3, 2, 4)).reshape(rows * count * tiles * 2, 128)
+    flag_rows = jnp.transpose(flags.reshape(rows, times, tiles, 128), (0, 2, 1, 3))
+    flag_rows = flag_rows.reshape(rows * tiles * times, 128)
 
     vmem = pl.BlockSpec(memory_space=pltpu.VMEM)
     hbm = pl.BlockSpec(memory_space=pl.ANY)
     dma = pltpu.SemaphoreType.DMA
-    own, mirrored, updated = pl.pallas_call(
+    residual, updated = pl.pallas_call(
         functools.partial(kernel, n_dir, n_freq, scaling),
         out_shape=(
-            jax.ShapeDtypeStruct((count, rows, stations), f32),
-            jax.ShapeDtypeStruct((count, rows, stations), f32),
+            jax.ShapeDtypeStruct((rows * count * tiles * 2, 128), f32),
             jax.ShapeDtypeStruct((local_dirs, stations), f32),
         ),
         in_specs=[
@@ -423,17 +430,20 @@
             vmem,
             vmem,
             vmem,
+            vmem,
             hbm,
             hbm,
             vmem,
             hbm,
         ],
-        out_specs=(vmem, vmem, vmem),
+        out_specs=(vmem, vmem),
         scratch_shapes=[
             pltpu.VMEM((count, 2, stations, sources), bf16),
+            pltpu.VMEM((rows * count * tiles * 2, 128), f32),
+            pltpu.VMEM((rows * tiles * times, 128), jnp.int32),
+            pltpu.VMEM((stations, stations), f32),
+            pltpu.VMEM((count, stations, 8), f32),
             pltpu.VMEM((count, rows, stations), f32),
-            pltpu.VMEM((times, rows, stations), f32),
-            pltpu.VMEM((stations, stations), f32),
             pltpu.VMEM((count, stations, 2 * sources), bf16),
             pltpu.VMEM((count, stations, 2 * sources), bf16),
             pltpu.VMEM((count, chips, 2, rows, stations), f32),
@@ -448,7 +458,7 @@
             pltpu.VMEM((local_dirs, 8, stations), f32),
             pltpu.VMEM((n_freq, 8, stations), f32),
             pltpu.VMEM((n_dir, 8, 128), f32),
-            pltpu.VMEM((128, stations), f32),
+            pltpu.VMEM((count, tiles, 128, 128), f32),
             dma((count,)),
             dma((3,)),
             dma((count,)),
@@ -470,16 +480,17 @@
     )(
         freq_ratio[None],
         gain,
-        cols,
-        src,
-        dirs,
-        kobs,
-        keep,
+        station_uv,
+        source_lm,
+        source_flux[None],
+        source_direction[None],
+        obs,
+        flag_rows,
         screen,
         screen_kernel,
     )
-    residual = jnp.stack([(own + mirrored) * 0.5, (own - mirrored) * 0.5], axis=1)
-    residual = jnp.transpose(residual, (2, 0, 1, 3))
+    residual = residual.reshape(rows, count, tiles, 2, 128)
+    residual = jnp.transpose(residual, (0, 1, 3, 2, 4))
     return (residual.reshape(observed.shape), updated)
 
 

time: 65.6 us -> 56.4 us (0.86)
  other arithmetic: 8.16 us -> 0 us
    mul x4 -> x0, other arithmetic: 2.67 us -> none  [the longest x1 1.01 us: body(): keep = jnp.transpose(flags, (1, 0, 2)).astype(f32) * cross.astype(f32)[None]]
    add x2 -> x0, other arithmetic: 2.64 us -> none  [the longest x1 2.63 us: body(): observed[:, :, :, 0] + observed[:, :, :, 1]]
    another operation x2 -> x0, other arithmetic: 1.47 us -> none  [body(): jnp.stack([(own + mirrored) * 0.5, (own - mirrored) * 0.5], axis=1)]
    unnamed x6 -> x2, local copies, waits for them, and re-layouts: 2.38 us -> 3.83 us
    concatenate x2 -> x0, other arithmetic: 1.31 us -> none  [the longest x1 1.29 us: body(): src = jnp.concatenate([source_lm, jnp.sqrt(source_flux)[None]], axis=0)]
    transpose x1 -> x0, local copies, waits for them, and re-layouts: 1.05 us -> none  [body(): cols = jnp.transpose(cols, (0, 2, 1))]
    sqrt x1 -> x0, local copies, waits for them, and re-layouts: 0.69 us -> none  [body(): src = jnp.concatenate([source_lm, jnp.sqrt(source_flux)[None]], axis=0)]
    broadcast_in_dim x3 -> x2, local copies, waits for them, and re-layouts: 2.01 us -> 2.49 us  [the longest x1 1.25 us: body(): source_flux[None]]
where the time goes in v2:
time: 56.4 us; the launch traced here: 56.1 us
  Pallas kernels  49.2 us (87%)
  local copies, waits for them, and re-layouts  6.32 us (11%)
  between operations  0.64 us (1%)
    pallas_call x1, Pallas kernels, body(): pl.pallas_call(functools.partial(kernel, n_dir, n_freq, scaling), out_sha...  49.2 us
    unnamed x2, local copies, waits for them, and re-layouts  3.83 us
    broadcast_in_dim x1, local copies, waits for them, and re-layouts, body(): source_flux[None]  1.25 us
    broadcast_in_dim x1, local copies, waits for them, and re-layouts, body(): source_direction[None]  1.24 us

profile of v2, /device:TPU:0, one launch (start us, length us, event | category | flops | bytes accessed | tf_op | source)
XLA Modules:
  0.0 56.1 jit_solution(17692563595723092677)
XLA Ops:
  0.6 1.2 %broadcast_in_dim.10.flux_ref = f32[1,384]{1,0:T(1,128)} reshape(f32[384]{0:T(512)} %param.16) | data formatting | bytes 3072 | tf_op jit(solution)/shard_map/broadcast_in_dim | solution.py:485
  1.9 1.2 %broadcast_in_dim.11.dirs_ref = s32[1,384]{1,0:T(1,128)} reshape(s32[384]{0:T(512)} %param.18) | data formatting | bytes 3072 | tf_op jit(solution)/shard_map/broadcast_in_dim | solution.py:486
  3.1 49.2 %calibrate.1 = (f32[2048,128]{1,0:T(8,128)}, f32[2,512]{1,0:T(2,128)}) custom-call(f32[1,2]{1,0:T(1,128)} %bitcast.21, bf16[4,2,512,384]{3,2,1,0:T(8,128)(2,1)} %bitcast.17, f32[2,2,512]{2,1,0:T(2,128)} %uv_ref.1, f32[2,384]{1,0:T(2,128)} %lm_ref.1, f32[1,384]{1,0:T(1,128)} %broadcast_in_dim.10.flux_ref, s32[1,384]{1,0:T(1,128)} %broadcast_in_dim.11.dirs_ref, ...), custom_call_target="tpu_custom_call" | custom-call | tf_op jit(solution)/shard_map/calibrate/pallas_call | solution.py:421
  52.3 2.6 %copy.17 = f32[64,2,2,2,512]{4,3,2,1,0:T(2,128)} copy(f32[64,2,2,2,512]{4,3,2,1,0:T(2,128)} %bitcast.18) | data formatting | bytes 2097152
  54.9 1.3 %copy.18 = f32[2,512]{1,0:T(2,128)} copy(f32[2,512]{1,0:T(2,128)} %get-tuple-element.9) | data formatting | bytes 8192

commit v3 on v2

--- a/solution.py
+++ b/solution.py
@@ -77,7 +77,7 @@
     sq_recv,
 ):
     count, _, stations, sources = gain.shape
-    local_dirs = pdir.shape[0]
+    local_dirs = pdir.shape[1]
     times = uv_ref.shape[0]
     rows = own_res.shape[1]
     tiles = stations // 128
@@ -168,11 +168,11 @@
             turns = col[:, 0:1] * lm[0:1] + col[:, 1:2] * lm[1:2]
             own = jnp.broadcast_to(col[:, 2:3], turns.shape)
             for d in range(1, local_dirs):
-                own = jnp.where(dirs_ref[...] == d, col[:, 2 + d : 3 + d], own)
+                own = jnp.where(dirs_ref[...][None] == d, col[:, 2 + d : 3 + d], own)
             turns = turns + own
             r = turns - jnp.round(turns)
             z = r * r
-            amp = jnp.sqrt(flux_ref[...])
+            amp = jnp.sqrt(flux_ref[...])[None]
             sine = horner(SIN_POLY, z) * (r * amp)
             cosine = horner(COS_POLY, z) * amp
             g_re = gain[m, 0, at, :].astype(f32)
@@ -241,9 +241,9 @@
 
     def direction_models(m):
         for d in range(local_dirs):
-            mask = jnp.where(dirs_ref[...] == d, 1.0, 0.0).astype(bf16)
+            mask = jnp.where(dirs_ref[...][None] == d, 1.0, 0.0).astype(bf16)
             mask = jnp.concatenate([mask, mask], axis=1)
-            pdir[d] = nt_dot(left[m] * mask, mixed[m])
+            pdir[m, d] = nt_dot(left[m] * mask, mixed[m])
 
     def local_grad(m):
         ag_copy(m, 0).wait_recv()
@@ -256,7 +256,7 @@
             u = ugath[m, at, :].astype(f32) * weight
             out = []
             for d in range(local_dirs):
-                w = u * pdir[d, at, :]
+                w = u * pdir[m, d, at, :]
                 part = w[:, 0:128]
                 for b in range(1, stations // 128):
                     part = part + w[:, b * 128 : (b + 1) * 128]
@@ -272,43 +272,72 @@
         for d in range(local_dirs):
             colacc[d] = out[d]
 
-    def step(s, _):
-        @pl.when(s < count)
-        def _():
-            phasors(s)
-            partial_model(s)
-
-            @pl.when(s == 0)
+    group = 128 // rows
+    lane0 = pl.multiple_of(lax.div(me, group) * 128, 128)
+    sub0 = pl.multiple_of(lax.rem(me, group) * rows, rows)
+
+    def mirror(m):
+        for b in range(tiles):
+            block = ugath[m, b * 128 : (b + 1) * 128, pl.ds(lane0, 128)].astype(f32)
+            tbuf[m, b] = jnp.transpose(block)
+        for b in range(tiles):
+            turned = tbuf[m, b, pl.ds(sub0, rows), :]
+            own = own_res[m, :, b * 128 : (b + 1) * 128]
+            at = (m * tiles + b) * 2
+            resid_ref[pl.ds(at, rows, stride=count * tiles * 2), :] = (own + turned) * 0.5
+            resid_ref[pl.ds(at + 1, rows, stride=count * tiles * 2), :] = (own - turned) * 0.5
+
+    lag = min(3, count - 1)
+
+    def build(s, _):
+        phasors(s)
+        partial_model(s)
+
+        @pl.when(s == 0)
+        def _():
+            pl.semaphore_wait(barrier, n_dir - 1 + n_freq - 1)
+            for c in in_copies:
+                c.wait()
+
+        s1_copy(s).start()
+
+        @pl.when(s >= 1)
+        def _():
+            chip_sum(s - 1)
+
+        @pl.when(s >= lag)
+        def _():
+            own_residual(s - lag)
+
+        return 0
+
+    lax.fori_loop(0, count, build, 0)
+    chip_sum(count - 1)
+
+    def spread(j, _):
+        @pl.when(j < lag)
+        def _():
+            own_residual(j + count - lag)
+
+        @pl.when(j < count)
+        def _():
+            direction_models(j)
+
+        @pl.when(jnp.logical_and(j >= 1, j < count + 1))
+        def _():
+            forward(j - 1)
+
+        @pl.when(j >= 2)
+        def _():
+            local_grad(j - 2)
+
+            @pl.when(j < count + 1)
             def _():
-                pl.semaphore_wait(barrier, n_dir - 1 + n_freq - 1)
-                for c in in_copies:
-                    c.wait()
-
-            s1_copy(s).start()
-
-        @pl.when(jnp.logical_and(s >= 1, s < count + 1))
-        def _():
-            chip_sum(s - 1)
-
-        @pl.when(jnp.logical_and(s >= 2, s < count + 2))
-        def _():
-            own_residual(s - 2)
-
-        @pl.when(jnp.logical_and(s >= 3, s < count + 3))
-        def _():
-            forward(s - 3)
-
-        @pl.when(s >= 4)
-        def _():
-            local_grad(s - 4)
-
-        @pl.when(jnp.logical_and(s >= 3, s < count + 3))
-        def _():
-            direction_models(s - 3)
+                mirror(j - 2)
 
         return 0
 
-    lax.fori_loop(0, count + 4, step, 0)
+    lax.fori_loop(0, count + 2, spread, 0)
 
     mine = []
     for d in range(local_dirs):
@@ -327,19 +356,7 @@
     for o in range(1, n_freq):
         fr_copy(o).start()
 
-    group = 128 // rows
-    lane0 = pl.multiple_of(lax.div(me, group) * 128, 128)
-    sub0 = pl.multiple_of(lax.rem(me, group) * rows, rows)
-
-    for m in range(count):
-        for b in range(tiles):
-            block = ugath[m, b * 128 : (b + 1) * 128, pl.ds(lane0, 128)].astype(f32)
-            tbuf[m, b] = jnp.transpose(block)
-            turned = tbuf[m, b, pl.ds(sub0, rows), :]
-            own = own_res[m, :, b * 128 : (b + 1) * 128]
-            at = (m * tiles + b) * 2
-            resid_ref[pl.ds(at, rows, stride=count * tiles * 2), :] = (own + turned) * 0.5
-            resid_ref[pl.ds(at + 1, rows, stride=count * tiles * 2), :] = (own - turned) * 0.5
+    mirror(count - 1)
 
     for o in range(1, n_freq):
         fr_copy(o).wait_recv()
@@ -447,7 +464,7 @@
             pltpu.VMEM((count, stations, 2 * sources), bf16),
             pltpu.VMEM((count, stations, 2 * sources), bf16),
             pltpu.VMEM((count, chips, 2, rows, stations), f32),
-            pltpu.VMEM((local_dirs, stations, stations), f32),
+            pltpu.VMEM((count, local_dirs, stations, stations), f32),
             pltpu.VMEM((count, chips, rows, stations), bf16),
             pltpu.VMEM((count, chips, rows, stations), bf16),
             pltpu.VMEM((count, chips, rows, stations), bf16),
@@ -482,8 +499,8 @@
         gain,
         station_uv,
         source_lm,
-        source_flux[None],
-        source_direction[None],
+        source_flux,
+        source_direction,
         obs,
         flag_rows,
         screen,

time: 56.4 us -> 53.8 us (0.954)
  local copies, waits for them, and re-layouts: 6.32 us -> 3.83 us
    broadcast_in_dim x2 -> x0, local copies, waits for them, and re-layouts: 2.49 us -> none  [the longest x1 1.25 us: body(): source_flux[None]]
where the time goes in v3:
time: 53.8 us; the launch traced here: 53.6 us
  Pallas kernels  49.1 us (91%)
  local copies, waits for them, and re-layouts  3.83 us (7%)
  between operations  0.64 us (1%)
    pallas_call x1, Pallas kernels, body(): pl.pallas_call(functools.partial(kernel, n_dir, n_freq, scaling), out_sha...  49.1 us
    unnamed x2, local copies, waits for them, and re-layouts  3.83 us

profile of v3, /device:TPU:0, one launch (start us, length us, event | category | flops | bytes accessed | tf_op | source)
XLA Modules:
  0.0 53.6 jit_solution(17157789786832604878)
XLA Ops:
  0.6 49.1 %calibrate.1 = (f32[2048,128]{1,0:T(8,128)}, f32[2,512]{1,0:T(2,128)}) custom-call(f32[1,2]{1,0:T(1,128)} %bitcast.21, bf16[4,2,512,384]{3,2,1,0:T(8,128)(2,1)} %bitcast.17, f32[2,2,512]{2,1,0:T(2,128)} %uv_ref.1, f32[2,384]{1,0:T(2,128)} %lm_ref.1, f32[384]{0:T(512)} %flux_ref.1, s32[384]{0:T(512)} %dirs_ref.1, f32[2048,128]{1,0:T(8,128)} %bitcast.19, ...), custom_call_target="tpu_custom_call" | custom-call | tf_op jit(solution)/shard_map/calibrate/pallas_call | solution.py:438
  49.8 2.6 %copy.17 = f32[64,2,2,2,512]{4,3,2,1,0:T(2,128)} copy(f32[64,2,2,2,512]{4,3,2,1,0:T(2,128)} %bitcast.18) | data formatting | bytes 2097152
  52.3 1.3 %copy.18 = f32[2,512]{1,0:T(2,128)} copy(f32[2,512]{1,0:T(2,128)} %get-tuple-element.9) | data formatting | bytes 8192

commit v4 on v3

--- a/solution.py
+++ b/solution.py
@@ -14,8 +14,8 @@
 f32 = jnp.float32
 bf16 = jnp.bfloat16
 
-SIN_POLY = (6.283185272722381, -41.341697068949564, 81.60502462236155, -76.70155117323625, 42.01616580115987, -14.868610927638132, 3.19969357384433)
-COS_POLY = (0.9999999891722522, -19.739204532086525, 64.93911898351571, -85.45016554378464, 60.16783168053616, -25.968313120273056, 6.5296101719799085)
+SIN_POLY = (6.283182818548967, -41.34142139850843, 81.59618386869336, -76.58010048367296, 41.20539468675213, -12.27126208031411)
+COS_POLY = (0.9999992215699194, -19.738982515967884, 64.92872660466796, -85.27239684712507, 58.79403796941139, -21.076780928848983)
 
 
 def horner(coefs, z):
@@ -87,6 +87,12 @@
     core = lax.rem(me, 2)
     chip = lax.div(me, 2)
     partner = chip * 2 + 1 - core
+    square = chips == 4
+    across = chip + 1 - 2 * lax.rem(chip, 2)
+    along = lax.rem(chip + 2, 4)
+    first = across + core * (along - across)
+    second = along + core * (across - along)
+    corner = 3 - chip
 
     def gain_copy(m):
         return pltpu.make_async_copy(gain_hbm.at[m], gain.at[m], gain_sem.at[m])
@@ -133,27 +139,39 @@
         return remote(s1buf.at[m], r1buf.at[m], s1_send.at[m], s1_recv.at[m], "dir", partner)
 
     def s2_copy(m, o):
-        to = lax.rem(chip + o, chips)
-        return remote(
-            s2buf.at[m, to],
-            r2buf.at[m, o],
-            s2_send.at[m, o],
-            s2_recv.at[m, o],
-            "dir",
-            to * 2 + core,
-        )
+        if square:
+            src, dst = s2buf.at[m, pl.ds(0, 2)], r2buf.at[m, pl.ds(0, 2)]
+            if o == 2:
+                src, dst = s2buf.at[m, 2], r2buf.at[m, 2]
+            to = first if o == 1 else second
+        else:
+            to = lax.rem(chip + o, chips)
+            src, dst = s2buf.at[m, to], r2buf.at[m, o]
+        return remote(src, dst, s2_send.at[m, o], s2_recv.at[m, o], "dir", to * 2 + core)
+
+    s2_count = 3 if square else chips
 
     def row_slice(owner):
         return pl.ds(pl.multiple_of(owner * rows, rows), rows)
 
+    def source_chip(o):
+        if square:
+            return (chip, first, second, corner)[o]
+        return lax.rem(chip - o + chips, chips)
+
     def ag_copy(m, o):
-        to = partner if o == 0 else lax.rem(chip + o, chips) * 2 + core
-        piece = ugath.at[m, row_slice(me), :]
+        owner = chip
+        if square:
+            to = (None, first, second, second)[o]
+            owner = first if o == 3 else chip
+        else:
+            to = lax.rem(chip + o, chips)
+        to = partner if o == 0 else to * 2 + core
+        piece = ugath.at[m, row_slice(owner * 2 + core), :]
         return remote(piece, piece, ag_send.at[m, o], ag_recv.at[m, o], "dir", to)
 
     def fw_copy(m, o):
-        owner = lax.rem(chip - o + chips, chips) * 2 + core
-        piece = ugath.at[m, row_slice(owner), :]
+        piece = ugath.at[m, row_slice(source_chip(o) * 2 + core), :]
         return remote(piece, piece, fw_send.at[m, o], ag_recv.at[m, chips + o - 1], "dir", partner)
 
     chunk = 32
@@ -181,10 +199,8 @@
             im = (g_re * sine + g_im * cosine).astype(bf16)
             left[m, at, :sources] = re
             left[m, at, sources:] = im
-            re = re.astype(f32)
-            im = im.astype(f32)
-            mixed[m, at, :sources] = (re + im).astype(bf16)
-            mixed[m, at, sources:] = (im - re).astype(bf16)
+            mixed[m, at, :sources] = re + im
+            mixed[m, at, sources:] = im - re
             return 0
 
         lax.fori_loop(0, stations // chunk, one, 0)
@@ -201,22 +217,33 @@
 
         lax.fori_loop(0, chips, one, 0)
 
+    def core_sum(m, j):
+        return pfull[m, j, core] + r1buf[m, j].astype(f32)
+
     def chip_sum(m):
         s1_copy(m).wait_recv()
-
-        def one(j, _):
-            total = pfull[m, j, core] + r1buf[m, j].astype(f32)
-            s2buf[m, j] = total.astype(bf16)
-            return 0
-
-        lax.fori_loop(0, chips, one, 0)
-        for o in range(1, chips):
-            s2_copy(m, o).start()
-        qown[m] = pfull[m, chip, core] + r1buf[m, chip].astype(f32)
+        if square:
+            s2buf[m, 0] = core_sum(m, first).astype(bf16)
+            s2buf[m, 1] = core_sum(m, corner).astype(bf16)
+            s2_copy(m, 1).start()
+            qown[m, 0] = core_sum(m, chip)
+            qown[m, 1] = core_sum(m, second)
+        else:
+            for j in range(chips):
+                s2buf[m, j] = core_sum(m, j).astype(bf16)
+            for o in range(1, chips):
+                s2_copy(m, o).start()
+            qown[m, 0] = core_sum(m, chip)
+
+    def square_sum(m):
+        s2_copy(m, 1).wait_recv()
+        s2buf[m, 2] = (qown[m, 1] + r2buf[m, 1].astype(f32)).astype(bf16)
+        s2_copy(m, 2).start()
+        qown[m, 0] = qown[m, 0] + r2buf[m, 0].astype(f32)
 
     def own_residual(m):
-        total = qown[m]
-        for o in range(1, chips):
+        total = qown[m, 0]
+        for o in [2] if square else range(1, chips):
             s2_copy(m, o).wait_recv()
             total = total + r2buf[m, o].astype(f32)
         row_ids = me * rows + lax.broadcasted_iota(jnp.int32, (rows, 128), 0)
@@ -231,11 +258,18 @@
             value = keep * (real + imag - total[:, lanes] * scaling)
             own_res[m, :, lanes] = value
             ugath[m, row_slice(me), lanes] = value.astype(bf16)
-        for o in list(range(1, chips)) + [0]:
+        for o in [1, 2, 0] if square else list(range(1, chips)) + [0]:
             ag_copy(m, o).start()
 
+    def relay(m):
+        ag_copy(m, 1).wait_recv()
+        ag_copy(m, 3).start()
+        fw_copy(m, 1).start()
+        ag_copy(m, 2).wait_recv()
+        fw_copy(m, 2).start()
+
     def forward(m):
-        for o in range(1, chips):
+        for o in [3] if square else range(1, chips):
             ag_copy(m, o).wait_recv()
             fw_copy(m, o).start()
 
@@ -287,57 +321,42 @@
             resid_ref[pl.ds(at, rows, stride=count * tiles * 2), :] = (own + turned) * 0.5
             resid_ref[pl.ds(at + 1, rows, stride=count * tiles * 2), :] = (own - turned) * 0.5
 
-    lag = min(3, count - 1)
-
-    def build(s, _):
-        phasors(s)
-        partial_model(s)
-
-        @pl.when(s == 0)
+    def step(s, _):
+        def stage(lag, run):
+            @pl.when(jnp.logical_and(s >= lag, s < count + lag))
+            def _():
+                run(s - lag)
+
+        @pl.when(s < count)
         def _():
-            pl.semaphore_wait(barrier, n_dir - 1 + n_freq - 1)
-            for c in in_copies:
-                c.wait()
-
-        s1_copy(s).start()
-
-        @pl.when(s >= 1)
+            phasors(s)
+            partial_model(s)
+
+            @pl.when(s == 0)
+            def _():
+                pl.semaphore_wait(barrier, n_dir - 1 + n_freq - 1)
+                for c in in_copies:
+                    c.wait()
+
+            s1_copy(s).start()
+
+        stage(1, chip_sum)
+        if square:
+            stage(2, square_sum)
+        stage(3, own_residual)
+        if square:
+            stage(5, relay)
+        stage(6, forward)
+        stage(7, local_grad)
+        stage(4, direction_models)
+
+        @pl.when(jnp.logical_and(s >= 7, s < count + 6))
         def _():
-            chip_sum(s - 1)
-
-        @pl.when(s >= lag)
-        def _():
-            own_residual(s - lag)
+            mirror(s - 7)
 
         return 0
 
-    lax.fori_loop(0, count, build, 0)
-    chip_sum(count - 1)
-
-    def spread(j, _):
-        @pl.when(j < lag)
-        def _():
-            own_residual(j + count - lag)
-
-        @pl.when(j < count)
-        def _():
-            direction_models(j)
-
-        @pl.when(jnp.logical_and(j >= 1, j < count + 1))
-        def _():
-            forward(j - 1)
-
-        @pl.when(j >= 2)
-        def _():
-            local_grad(j - 2)
-
-            @pl.when(j < count + 1)
-            def _():
-                mirror(j - 2)
-
-        return 0
-
-    lax.fori_loop(0, count + 2, spread, 0)
+    lax.fori_loop(0, count + 7, step, 0)
 
     mine = []
     for d in range(local_dirs):
@@ -388,8 +407,9 @@
 
     def drain(m, _):
         s1_copy(m).wait_send()
+        for o in range(1, s2_count):
+            s2_copy(m, o).wait_send()
         for o in range(1, chips):
-            s2_copy(m, o).wait_send()
             fw_copy(m, o).wait_send()
         for o in range(chips):
             ag_copy(m, o).wait_send()
@@ -468,7 +488,7 @@
             pltpu.VMEM((count, chips, rows, stations), bf16),
             pltpu.VMEM((count, chips, rows, stations), bf16),
             pltpu.VMEM((count, chips, rows, stations), bf16),
-            pltpu.VMEM((count, rows, stations), f32),
+            pltpu.VMEM((count, 2, rows, stations), f32),
             pltpu.VMEM((count, chips, rows, stations), bf16),
             pltpu.VMEM((count, stations, stations), bf16),
             pltpu.VMEM((local_dirs, stations, 128), f32),

time: 53.8 us -> 55.4 us (1.030)
  Pallas kernels: 49.1 us -> 50.7 us
    pallas_call x1, Pallas kernels: 49.1 us -> 50.7 us  [body(): pl.pallas_call(functools.partial(kernel, n_dir, n_freq, scaling), out_sha...]
where the time goes in v4:
time: 55.4 us; the launch traced here: 55.1 us
  Pallas kernels  50.7 us (92%)
  local copies, waits for them, and re-layouts  3.83 us (7%)
  between operations  0.64 us (1%)
    pallas_call x1, Pallas kernels, body(): pl.pallas_call(functools.partial(kernel, n_dir, n_freq, scaling), out_sha...  50.7 us
    unnamed x2, local copies, waits for them, and re-layouts  3.83 us

profile of v4, /device:TPU:0, one launch (start us, length us, event | category | flops | bytes accessed | tf_op | source)
XLA Modules:
  0.0 55.1 jit_solution(1469757345706215440)
XLA Ops:
  0.6 50.7 %calibrate.1 = (f32[2048,128]{1,0:T(8,128)}, f32[2,512]{1,0:T(2,128)}) custom-call(f32[1,2]{1,0:T(1,128)} %bitcast.21, bf16[4,2,512,384]{3,2,1,0:T(8,128)(2,1)} %bitcast.17, f32[2,2,512]{2,1,0:T(2,128)} %uv_ref.1, f32[2,384]{1,0:T(2,128)} %lm_ref.1, f32[384]{0:T(512)} %flux_ref.1, s32[384]{0:T(512)} %dirs_ref.1, f32[2048,128]{1,0:T(8,128)} %bitcast.19, ...), custom_call_target="tpu_custom_call" | custom-call | tf_op jit(solution)/shard_map/calibrate/pallas_call | solution.py:458
  51.3 2.6 %copy.17 = f32[64,2,2,2,512]{4,3,2,1,0:T(2,128)} copy(f32[64,2,2,2,512]{4,3,2,1,0:T(2,128)} %bitcast.18) | data formatting | bytes 2097152
  53.9 1.3 %copy.18 = f32[2,512]{1,0:T(2,128)} copy(f32[2,512]{1,0:T(2,128)} %get-tuple-element.9) | data formatting | bytes 8192

commit v5 on v3

--- a/solution.py
+++ b/solution.py
@@ -14,8 +14,8 @@
 f32 = jnp.float32
 bf16 = jnp.bfloat16
 
-SIN_POLY = (6.283185272722381, -41.341697068949564, 81.60502462236155, -76.70155117323625, 42.01616580115987, -14.868610927638132, 3.19969357384433)
-COS_POLY = (0.9999999891722522, -19.739204532086525, 64.93911898351571, -85.45016554378464, 60.16783168053616, -25.968313120273056, 6.5296101719799085)
+SIN_POLY = (6.283182818548967, -41.34142139850843, 81.59618386869336, -76.58010048367296, 41.20539468675213, -12.27126208031411)
+COS_POLY = (0.9999992215699194, -19.738982515967884, 64.92872660466796, -85.27239684712507, 58.79403796941139, -21.076780928848983)
 
 
 def horner(coefs, z):
@@ -181,10 +181,8 @@
             im = (g_re * sine + g_im * cosine).astype(bf16)
             left[m, at, :sources] = re
             left[m, at, sources:] = im
-            re = re.astype(f32)
-            im = im.astype(f32)
-            mixed[m, at, :sources] = (re + im).astype(bf16)
-            mixed[m, at, sources:] = (im - re).astype(bf16)
+            mixed[m, at, :sources] = re + im
+            mixed[m, at, sources:] = im - re
             return 0
 
         lax.fori_loop(0, stations // chunk, one, 0)
@@ -319,13 +317,13 @@
         def _():
             own_residual(j + count - lag)
 
+        @pl.when(jnp.logical_and(j >= 1, j < count + 1))
+        def _():
+            forward(j - 1)
+
         @pl.when(j < count)
         def _():
             direction_models(j)
-
-        @pl.when(jnp.logical_and(j >= 1, j < count + 1))
-        def _():
-            forward(j - 1)
 
         @pl.when(j >= 2)
         def _():

time: 53.8 us -> 53 us (0.985)
  Pallas kernels: 49.1 us -> 48.3 us
    pallas_call x1, Pallas kernels: 49.1 us -> 48.3 us  [body(): pl.pallas_call(functools.partial(kernel, n_dir, n_freq, scaling), out_sha...]
where the time goes in v5:
time: 53 us; the launch traced here: 52.8 us
  Pallas kernels  48.3 us (91%)
  local copies, waits for them, and re-layouts  3.83 us (7%)
  between operations  0.64 us (1%)
    pallas_call x1, Pallas kernels, body(): pl.pallas_call(functools.partial(kernel, n_dir, n_freq, scaling), out_sha...  48.3 us
    unnamed x2, local copies, waits for them, and re-layouts  3.83 us

profile of v5, /device:TPU:0, one launch (start us, length us, event | category | flops | bytes accessed | tf_op | source)
XLA Modules:
  0.0 52.8 jit_solution(11654648537026858556)
XLA Ops:
  0.6 48.3 %calibrate.1 = (f32[2048,128]{1,0:T(8,128)}, f32[2,512]{1,0:T(2,128)}) custom-call(f32[1,2]{1,0:T(1,128)} %bitcast.21, bf16[4,2,512,384]{3,2,1,0:T(8,128)(2,1)} %bitcast.17, f32[2,2,512]{2,1,0:T(2,128)} %uv_ref.1, f32[2,384]{1,0:T(2,128)} %lm_ref.1, f32[384]{0:T(512)} %flux_ref.1, s32[384]{0:T(512)} %dirs_ref.1, f32[2048,128]{1,0:T(8,128)} %bitcast.19, ...), custom_call_target="tpu_custom_call" | custom-call | tf_op jit(solution)/shard_map/calibrate/pallas_call | solution.py:436
  48.9 2.6 %copy.17 = f32[64,2,2,2,512]{4,3,2,1,0:T(2,128)} copy(f32[64,2,2,2,512]{4,3,2,1,0:T(2,128)} %bitcast.18) | data formatting | bytes 2097152
  51.5 1.3 %copy.18 = f32[2,512]{1,0:T(2,128)} copy(f32[2,512]{1,0:T(2,128)} %get-tuple-element.9) | data formatting | bytes 8192

commit v6 on v5

--- a/solution.py
+++ b/solution.py
@@ -398,6 +398,11 @@
         fr_copy(o).wait_send()
     for o in range(1, n_dir):
         sq_copy(o).wait_send()
+
+
+def hand_over(resid_ref, updated_ref, resid_out, updated_out):
+    resid_out[...] = resid_ref[...]
+    updated_out[...] = updated_ref[...]
 
 
 def body(
@@ -504,6 +509,20 @@
         screen,
         screen_kernel,
     )
+    halves = 2
+    block = pl.BlockSpec((residual.shape[0] // halves, 128), lambda i: (i, 0))
+    small = pl.BlockSpec((local_dirs, stations), lambda i: (0, 0))
+    residual, updated = pl.pallas_call(
+        hand_over,
+        grid=(halves,),
+        out_shape=(
+            jax.ShapeDtypeStruct(residual.shape, f32),
+            jax.ShapeDtypeStruct(updated.shape, f32),
+        ),
+        in_specs=[block, small],
+        out_specs=(block, small),
+        name="results",
+    )(residual, updated)
     residual = residual.reshape(rows, count, tiles, 2, 128)
     residual = jnp.transpose(residual, (0, 1, 3, 2, 4))
     return (residual.reshape(observed.shape), updated)

time: 53 us -> 51.2 us (0.966)
  local copies, waits for them, and re-layouts: 3.83 us -> 0 us
  Pallas kernels: 48.3 us -> 50.3 us
    unnamed x2 -> x0, local copies, waits for them, and re-layouts: 3.83 us -> none
    pallas_call x0 -> x1, Pallas kernels: none -> 2.06 us  [body(): pl.pallas_call(hand_over, grid=(halves,), out_shape=(jax.ShapeDtypeStruct...]
where the time goes in v6:
time: 51.2 us; the launch traced here: 51 us
  Pallas kernels  50.3 us (98%)
  between operations  0.64 us (1%)
    pallas_call x1, Pallas kernels, body(): pl.pallas_call(functools.partial(kernel, n_dir, n_freq, scaling), out_sha...  48.3 us
    pallas_call x1, Pallas kernels, body(): pl.pallas_call(hand_over, grid=(halves,), out_shape=(jax.ShapeDtypeStruct...  2.06 us

profile of v6, /device:TPU:0, one launch (start us, length us, event | category | flops | bytes accessed | tf_op | source)
XLA Modules:
  0.0 51.0 jit_solution(16866170854604411259)
XLA Ops:
  0.6 48.3 %calibrate.1 = (f32[2048,128]{1,0:T(8,128)}, f32[2,512]{1,0:T(2,128)}) custom-call(f32[1,2]{1,0:T(1,128)} %bitcast.20, bf16[4,2,512,384]{3,2,1,0:T(8,128)(2,1)} %bitcast.17, f32[2,2,512]{2,1,0:T(2,128)} %uv_ref.1, f32[2,384]{1,0:T(2,128)} %lm_ref.1, f32[384]{0:T(512)} %flux_ref.1, s32[384]{0:T(512)} %dirs_ref.1, f32[2048,128]{1,0:T(8,128)} %bitcast.18, ...), custom_call_target="tpu_custom_call" | custom-call | tf_op jit(solution)/shard_map/calibrate/pallas_call | solution.py:441
  48.9 2.1 %results.1 = (f32[2048,128]{1,0:T(8,128)}, f32[2,512]{1,0:T(2,128)}) custom-call(f32[2048,128]{1,0:T(8,128)} %get-tuple-element.6.resid_ref, f32[2,512]{1,0:T(2,128)} %get-tuple-element.7.updated_ref), custom_call_target="tpu_custom_call" | custom-call | tf_op jit(solution)/shard_map/results/pallas_call | solution.py:515
